TPU v7x, 128 devices: a whole 4x4x4 slice. The times are simulated.
128 devices in a mesh: grp: 4 (over y), cp: 32 (over x, z, core).
Axes of the slice: x: 4, y: 4, z: 4, core: 2. Of those that a mesh axis runs over, the one named last changes fastest.
Arguments:
- queries: bfloat16 [4, 16384, 4096], P(None, ('grp', 'cp')), may hold values from -6 to 6, as said below
- keys: bfloat16 [4, 16384, 1024], P(None, ('grp', 'cp')), may hold values from -6 to 6, as said below
- values: bfloat16 [4, 16384, 1024], P(None, ('grp', 'cp')), may hold values from -6 to 6
- doc_lengths: int32 [4, 16], replicated, may hold values from 1 to 4096, 16384 in all within a row
Outputs:
- attended: bfloat16 [4, 16384, 4096], P(None, ('grp', 'cp'))
Inputs may be any that keep to these rules, and one draw needn't show every extreme that they name: `doc_lengths`: each row holds the lengths of 16 documents that fill the stream's 16384 tokens exactly; the longest is exactly 4096 tokens. `queries`: entries of order one. `keys`: entries of order one.
All inputs are finite; a program needn't handle non-finite values.
Results may differ from a plain program's by a relative error of at most 0.0038.
Values may be sent and summed in bfloat16 or wider, within the bound.
No kernel may reach another device: no remote copies, remote signals or barrier semaphores. Data moves between devices by JAX's collectives and lax.ppermute only.
A program may use at most 128 MiB of HBM per device.

v0:
```python
import jax
import jax.numpy as jnp
from jax import lax
from jax.experimental import pallas as pl
from jax.experimental.pallas import tpu as pltpu
from jax.sharding import PartitionSpec as P

QUERY_HEADS = 32
KEY_VALUE_HEADS = 8
WIDTH = 128
DOCS = 16
BLOCK = 128
RANKS = 32
CHUNK = RANKS * BLOCK
PAD = 512
TILE = 256
TILES = CHUNK // TILE
EDGE = 512
COLUMNS = EDGE // WIDTH
FACTOR = WIDTH ** (-0.5) * 1.4426950408889634
NEGATIVE = -1e30
LEAST = -(2**31)
LOW, HIGH = 1e-30, 1e30


def pack_keys(k_ref, v_ref, out_ref):
    for head in range(KEY_VALUE_HEADS):
        columns = slice(head * WIDTH, (head + 1) * WIDTH)
        out_ref[0, head, 0, 0] = k_ref[0, :, columns].T
        out_ref[0, head, 0, 1] = v_ref[0, :, columns]


def pack_queries(q_ref, even_ref, odd_ref):
    for turn, out_ref in enumerate((even_ref, odd_ref)):
        for head in range(QUERY_HEADS):
            out_ref[0, head // 2, head % 2] = q_ref[turn, :, head * WIDTH : (head + 1) * WIDTH]


def unpack_outputs(even_ref, odd_ref, out_ref):
    for turn, in_ref in enumerate((even_ref, odd_ref)):
        for head in range(QUERY_HEADS):
            out_ref[turn, :, head * WIDTH : (head + 1) * WIDTH] = in_ref[0, head // 2, head % 2]


def attend(info, lengths, q_ref, mine, other, mine_before, other_before, o_ref, kbuf, vbuf, probs, acc, sums, portion, lows, reach, top, ends, low_of, whole_of, docs_of, span_of, arrived):
    core, plane, pair, turn = info[0], info[1], info[2], info[3]
    stream = pair * 2 + turn
    base = (plane - 1) * CHUNK

    def fetch(before, now):
        copies = [
            pltpu.make_async_copy(source.at[:, pl.ds(half * BLOCK, BLOCK)], target.at[pl.ds(first, RANKS)], arrived.at[number])
            for number, (source, half, target, first) in enumerate(
                (
                    (before, 0, kbuf, PAD // BLOCK),
                    (now, 0, kbuf, PAD // BLOCK + RANKS),
                    (before, 1, vbuf, PAD // BLOCK),
                    (now, 1, vbuf, PAD // BLOCK + RANKS),
                )
            )
        ]
        for copy in copies:
            copy.start()
        for copy in copies:
            copy.wait()

    @pl.when(turn == core)
    def _():
        fetch(mine_before, mine)

    @pl.when(turn != core)
    def _():
        fetch(other_before, other)

    rows = lax.broadcasted_iota(jnp.int32, (2, BLOCK, WIDTH), 0) * BLOCK + lax.broadcasted_iota(
        jnp.int32, (2, BLOCK, WIDTH), 1
    )
    lanes = lax.broadcasted_iota(jnp.int32, (2, BLOCK, WIDTH), 2)

    kbuf[: PAD // BLOCK] = jnp.zeros((PAD // BLOCK, WIDTH, BLOCK), jnp.bfloat16)
    vbuf[: PAD // BLOCK] = jnp.zeros((PAD // BLOCK, BLOCK, WIDTH), jnp.bfloat16)
    acc[...] = jnp.zeros_like(acc)
    sums[...] = jnp.zeros_like(sums)
    probs[...] = jnp.zeros_like(probs)

    total = -base
    for doc in range(DOCS):
        total = total + lengths[stream, doc]
        ends[doc] = total

    def top_of(tile):
        return CHUNK + (tile + 1) * TILE - EDGE

    def survey(tile, blocks):
        begin = CHUNK + tile * TILE
        first, last, passed, within = -base, -base, 0, 0
        for doc in range(DOCS):
            end = ends[doc]
            first = jnp.where(end <= begin, end, first)
            last = jnp.where(end < begin + TILE, end, last)
            passed += (end <= begin).astype(jnp.int32)
            within += (end < begin + TILE).astype(jnp.int32)
        low = (first // TILE) * TILE
        low_of[tile] = low
        whole_of[tile] = last
        docs_of[0, tile] = first
        docs_of[1, tile] = passed
        docs_of[2, tile] = within
        return blocks + (begin + TILE - low + EDGE - 1) // EDGE

    blocks = lax.fori_loop(0, TILES, survey, 0)

    def prepare(tile):
        begin = CHUNK + tile * TILE
        first = docs_of[0, tile]
        lows[...] = (first + LEAST) - lanes
        reach[...] = rows + (begin - first + LEAST)

        def mark(doc, carry):
            end = ends[doc]
            inside = rows + begin >= end
            lows[...] = jnp.where(inside, (end + LEAST) - lanes, lows[...])
            reach[...] = jnp.where(inside, rows + (begin - end + LEAST), reach[...])
            return carry

        lax.fori_loop(docs_of[1, tile], docs_of[2, tile], mark, 0)

    def scores_of(tile, offset):
        at = (offset + PAD) // BLOCK
        queries = q_ref[pl.ds(tile * 2, 2)].reshape(4 * BLOCK, WIDTH)
        return [
            jnp.dot(
                queries,
                jnp.concatenate([kbuf[at + column], kbuf[at + column + 1]], axis=1),
                preferred_element_type=jnp.float32,
            )
            for column in range(0, COLUMNS, 2)
        ]

    def weigh(found, offset, uses_mask):
        for block in range(2):
            for row in range(0, BLOCK, 16):
                if uses_mask:
                    allowed = [
                        (offset + column * WIDTH) - lows[block, row : row + 16] <= reach[block, row : row + 16]
                        for column in range(COLUMNS)
                    ]
                for head in range(2):
                    rows_at = (block * 2 + head) * BLOCK + row
                    parts = []
                    for column in range(COLUMNS):
                        lane = column % 2 * WIDTH
                        part = found[column // 2][rows_at : rows_at + 16, lane : lane + WIDTH] * FACTOR
                        if uses_mask:
                            part = jnp.where(allowed[column], part, NEGATIVE)
                        part = jnp.exp2(part)
                        probs[column, rows_at : rows_at + 16] = part.astype(jnp.bfloat16)
                        parts.append(part)
                    sums[rows_at : rows_at + 16] += (parts[0] + parts[1]) + (parts[2] + parts[3])

    def product_of(offset):
        values = vbuf[pl.ds((offset + PAD) // BLOCK, EDGE // BLOCK)].reshape(EDGE, WIDTH)
        return [
            jnp.dot(
                jnp.concatenate([probs[column, half : half + 2 * BLOCK] for column in range(COLUMNS)], axis=1),
                values,
                preferred_element_type=jnp.float32,
            )
            for half in (0, 2 * BLOCK)
        ]

    def add(products):
        for half in range(2):
            acc[half * 2 * BLOCK : (half + 1) * 2 * BLOCK] += products[half]

    def close():
        total = jnp.sum(sums[...], axis=-1, keepdims=True)
        span_of[0] = jnp.minimum(span_of[0], jnp.min(total.reshape(64, 8, 1), axis=0))
        span_of[1] = jnp.maximum(span_of[1], jnp.max(total.reshape(64, 8, 1), axis=0))
        portion[...] = jnp.broadcast_to(1.0 / total, (4 * BLOCK, WIDTH))
        sums[...] = jnp.zeros_like(sums)

    def finish(tile):
        o_ref[pl.ds(tile * 2, 2)] = (acc[...] * portion[...]).astype(jnp.bfloat16).reshape(2, 2, BLOCK, WIDTH)
        acc[...] = jnp.zeros_like(acc)

    def fast(step, carry):
        tile, offset, tile_before, offset_before, closes = carry

        def both(uses_mask):
            found = scores_of(tile, offset)
            products = product_of(offset_before)
            weigh(found, offset, uses_mask)
            add(products)

        plain = (offset >= whole_of[tile]) & (offset < top_of(tile))

        @pl.when(plain)
        def _():
            both(False)

        @pl.when(jnp.logical_not(plain))
        def _():
            both(True)

        @pl.when(closes == 1)
        def _():
            finish(tile_before)

        ended = (offset <= low_of[tile]).astype(jnp.int32)
        tile_next = jnp.minimum(tile + ended, TILES - 1)
        offset_next = jnp.where(ended == 1, top_of(tile_next), offset - EDGE)

        @pl.when(ended == 1)
        def _():
            close()
            prepare(tile_next)

        return tile_next, offset_next, tile, offset, ended

    def slow(tile, carry):
        begin = CHUNK + tile * TILE
        prepare(tile)
        acc[...] = jnp.zeros_like(acc)
        sums[...] = jnp.zeros_like(sums)
        top[...] = jnp.full_like(top, NEGATIVE)

        def absorb(step, carry):
            offset = top_of(tile) - step * EDGE
            found = scores_of(tile, offset)
            for piece in range(4):
                at = slice(piece * BLOCK, (piece + 1) * BLOCK)
                parts = []
                for column in range(COLUMNS):
                    lane = column % 2 * WIDTH
                    part = found[column // 2][at, lane : lane + WIDTH]
                    allowed = (offset + column * WIDTH) - lows[piece // 2] <= reach[piece // 2]
                    parts.append(jnp.where(allowed, part * FACTOR, NEGATIVE))
                before = top[at]
                highest = jnp.maximum(jnp.maximum(parts[0], parts[1]), jnp.maximum(parts[2], parts[3]))
                peak = jnp.maximum(before, jnp.max(highest, axis=-1, keepdims=True))
                shrink = jnp.exp2(before - peak)
                total = jnp.zeros((BLOCK, WIDTH), jnp.float32)
                for column in range(COLUMNS):
                    part = jnp.where(parts[column] > 0.5 * NEGATIVE, jnp.exp2(parts[column] - peak), 0.0)
                    probs[column, at] = part.astype(jnp.bfloat16)
                    total = total + part
                sums[at] = sums[at] * shrink + total
                acc[at] = acc[at] * shrink
                top[at] = peak
            add(product_of(offset))
            return carry

        lax.fori_loop(0, (begin + TILE - low_of[tile] + EDGE - 1) // EDGE, absorb, 0)
        close()
        finish(tile)
        return carry

    span_of[0] = jnp.full((8, WIDTH), 1.0, jnp.float32)
    span_of[1] = jnp.full((8, WIDTH), 1.0, jnp.float32)
    prepare(0)
    lax.fori_loop(0, blocks + 1, fast, (0, top_of(0), 0, top_of(0), 0))
    fits = (jnp.min(span_of[0]) >= LOW) & (jnp.max(span_of[1]) <= HIGH)

    @pl.when(jnp.logical_not(fits))
    def _():
        lax.fori_loop(0, TILES, slow, 0)


def estimate(flops, moved, powers=0):
    return pl.CostEstimate(flops=flops, bytes_accessed=moved, transcendentals=powers)


def attention(info, doc_lengths, *arrays):
    anywhere = pl.BlockSpec(memory_space=pl.ANY)
    half = pl.BlockSpec((RANKS, 2, BLOCK, WIDTH), lambda u, *_: (0, 0, 0, 0), pipeline_mode=pl.Buffered(1))
    return pl.pallas_call(
        attend,
        grid_spec=pltpu.PrefetchScalarGridSpec(
            num_scalar_prefetch=2,
            grid=(1,),
            in_specs=[half, anywhere, anywhere, anywhere, anywhere],
            out_specs=half,
            scratch_shapes=[
                pltpu.VMEM(((PAD + 2 * CHUNK) // BLOCK, WIDTH, BLOCK), jnp.bfloat16),
                pltpu.VMEM(((PAD + 2 * CHUNK) // BLOCK, BLOCK, WIDTH), jnp.bfloat16),
                pltpu.VMEM((COLUMNS, 4 * BLOCK, WIDTH), jnp.bfloat16),
                pltpu.VMEM((4 * BLOCK, WIDTH), jnp.float32),
                pltpu.VMEM((4 * BLOCK, WIDTH), jnp.float32),
                pltpu.VMEM((4 * BLOCK, WIDTH), jnp.float32),
                pltpu.VMEM((2, BLOCK, WIDTH), jnp.int32),
                pltpu.VMEM((2, BLOCK, WIDTH), jnp.int32),
                pltpu.VMEM((4 * BLOCK, WIDTH), jnp.float32),
                pltpu.SMEM((DOCS,), jnp.int32),
                pltpu.SMEM((TILES,), jnp.int32),
                pltpu.SMEM((TILES,), jnp.int32),
                pltpu.SMEM((3, TILES), jnp.int32),
                pltpu.VMEM((2, 8, WIDTH), jnp.float32),
                pltpu.SemaphoreType.DMA((4,)),
            ],
        ),
        out_shape=jax.ShapeDtypeStruct((RANKS, 2, BLOCK, WIDTH), jnp.bfloat16),
        cost_estimate=estimate(20 << 30, 8 << 20, 10 << 20),
        compiler_params=pltpu.CompilerParams(vmem_limit_bytes=60 << 20),
        name="attend",
    )(info, doc_lengths, *arrays)


def on_device(queries, keys, values, doc_lengths):
    rank = lax.axis_index("cp")
    plane = lax.axis_index("grp")
    bf16 = jnp.bfloat16

    packed_kv = pl.pallas_call(
        pack_keys,
        grid=(4,),
        in_specs=[pl.BlockSpec((1, BLOCK, KEY_VALUE_HEADS * WIDTH), lambda s: (s, 0, 0))] * 2,
        out_specs=pl.BlockSpec((1, 8, 1, 2, BLOCK, WIDTH), lambda s: (s // 2, 0, s % 2, 0, 0, 0)),
        out_shape=jax.ShapeDtypeStruct((2, 8, 2, 2, BLOCK, WIDTH), bf16),
        cost_estimate=estimate(0, 4 << 20),
        name="pack_keys",
    )(keys, values)
    packed_q = pl.pallas_call(
        pack_queries,
        grid=(2,),
        in_specs=[pl.BlockSpec((2, BLOCK, QUERY_HEADS * WIDTH), lambda p: (p, 0, 0))],
        out_specs=[pl.BlockSpec((1, 16, 2, BLOCK, WIDTH), lambda p: (p, 0, 0, 0, 0))] * 2,
        out_shape=[jax.ShapeDtypeStruct((2, 16, 2, BLOCK, WIDTH), bf16)] * 2,
        cost_estimate=estimate(0, 8 << 20),
        name="pack_queries",
    )(queries)

    swap = [(i, i ^ 1) for i in range(RANKS)]
    onward = [(i, (i + 1) % 4) for i in range(4)]
    mine = lax.all_to_all(packed_kv.reshape(RANKS, 2 * BLOCK, WIDTH), "cp", 0, 0, tiled=True)
    mine_before = lax.ppermute(mine, "grp", onward)
    other = lax.ppermute(mine, "cp", swap)
    got_q = []
    for packed in packed_q:
        got_q.append(lax.all_to_all(packed.reshape(RANKS, 2 * BLOCK, WIDTH), "cp", 0, 0, tiled=True))
    other_before = lax.ppermute(mine_before, "cp", swap)
    back = []
    for turn in range(2):
        info = jnp.stack([rank % 2, plane, rank // 16, turn]).astype(jnp.int32)
        result = attention(
            info, doc_lengths, got_q[turn].reshape(RANKS, 2, BLOCK, WIDTH), mine, other, mine_before, other_before
        )
        sent = lax.all_to_all(result.reshape(RANKS, 2 * BLOCK, WIDTH), "cp", 0, 0, tiled=True)
        back.append(sent.reshape(2, 16, 2, BLOCK, WIDTH))
    return pl.pallas_call(
        unpack_outputs,
        grid=(2,),
        in_specs=[pl.BlockSpec((1, 16, 2, BLOCK, WIDTH), lambda p: (p, 0, 0, 0, 0))] * 2,
        out_specs=pl.BlockSpec((2, BLOCK, QUERY_HEADS * WIDTH), lambda p: (p, 0, 0)),
        out_shape=jax.ShapeDtypeStruct((4, BLOCK, QUERY_HEADS * WIDTH), bf16),
        cost_estimate=estimate(0, 8 << 20),
        name="unpack_outputs",
    )(*back)


def solution(mesh):
    placed = P(None, ("grp", "cp"), None)
    return jax.shard_map(
        on_device,
        mesh=mesh,
        in_specs=(placed, placed, placed, P()),
        out_specs=placed,
        check_vma=False,
    )
```

profile of v0, /device:TPU:25, one launch (start us, length us, event | category | flops | bytes accessed | tf_op | source)
XLA Modules:
  0.0 319.3 jit_solution(10841504451328580066)
XLA Ops:
  0.0 4.0 %pack_keys.1 = bf16[2,8,2,2,128,128]{5,4,3,2,1,0:T(8,128)(2,1)} custom-call(bf16[4,128,1024]{2,1,0:T(8,128)(2,1)} %k_ref.1, bf16[4,128,1024]{2,1,0:T(8,128)(2,1)} %v_ref.1), custom_call_target="tpu_custom_call" | custom-call | bytes 4194304 | tf_op jit(solution)/shard_map/pack_keys/pallas_call | solution.py:314
  4.0 36.7 %all_to_all.25.mine = bf16[32,256,128]{2,1,0:T(8,128)(2,1)S(1)} all-to-all(bf16[32,256,128]{2,1,0:T(8,128)(2,1)} %bitcast.12), channel_id=1, replica_groups=mesh['grp'=4,'cp'=32] {'cp'}, dimensions={0} | all-to-all | bytes 4194304 | tf_op jit(solution)/shard_map/all_to_all | solution.py:335
  40.8 0.0 copy-start.1
  40.8 0.0 collective-permute-start.1
  40.8 4.7 %pack_queries.1 = (bf16[2,16,2,128,128]{4,3,2,1,0:T(8,128)(2,1)}, bf16[2,16,2,128,128]{4,3,2,1,0:T(8,128)(2,1)}) custom-call(bf16[4,128,4096]{2,1,0:T(8,128)(2,1)} %q_ref.1), custom_call_target="tpu_custom_call" | custom-call | bytes 8388608 | tf_op jit(solution)/shard_map/pack_queries/pallas_call | solution.py:323
  45.5 4.5 %all-to-all-start = ((bf16[32,256,128]{2,1,0:T(8,128)(2,1)}), bf16[32,256,128]{2,1,0:T(8,128)(2,1)}, u32[]{:S(2)}, u32[]{:S(2)}) async-start(bf16[32,256,128]{2,1,0:T(8,128)(2,1)} %bitcast.16), calls=%async_computation | async-start | bytes 4194304 | tf_op jit(solution)/shard_map/all_to_all | solution.py:340
  50.0 0.0 copy-done.1
  50.1 0.4 collective-permute-start
  50.5 37.5 %collective-permute-done.1.mine_before = bf16[32,256,128]{2,1,0:T(8,128)(2,1)} collective-permute-done((bf16[32,256,128]{2,1,0:T(8,128)(2,1)S(1)}, bf16[32,256,128]{2,1,0:T(8,128)(2,1)}, u32[]{:S(2)}, u32[]{:S(2)}) %collective-permute-start.1) | collective-permute-done | bytes 2097184 | tf_op jit(solution)/shard_map/ppermute | solution.py:336
  88.0 1.0 collective-permute-start.2
  88.9 0.7 pad_add_fusion.2
  89.6 0.0 all-to-all-done
  89.6 4.6 %all-to-all-start.3 = ((bf16[32,256,128]{2,1,0:T(8,128)(2,1)}), bf16[32,256,128]{2,1,0:T(8,128)(2,1)}, u32[]{:S(2)}, u32[]{:S(2)}) async-start(bf16[32,256,128]{2,1,0:T(8,128)(2,1)} %bitcast.15), calls=%async_computation.3 | async-start | bytes 4194304 | tf_op jit(solution)/shard_map/all_to_all | solution.py:340
  94.2 0.7 pad_add_fusion.info
  94.8 0.0 collective-permute-done.other
  94.8 0.0 collective-permute-done.2.other_before
  94.8 111.6 %attend.2 = bf16[32,2,128,128]{3,2,1,0:T(8,128)(2,1)} custom-call(s32[4]{0:T(128)} %pad_add_fusion.info, s32[4,16]{1,0:T(4,128)} %lengths.3, bf16[32,2,128,128]{3,2,1,0:T(8,128)(2,1)} %bitcast.4.q_ref, bf16[32,256,128]{2,1,0:T(8,128)(2,1)} %copy-done.1, bf16[32,256,128]{2,1,0:T(8,128)(2,1)} %collective-permute-done.other, ...), custom_call_target="tpu_custom_call" | custom-call | flops 21474836480 | bytes 8388608 | tf_op jit(solution)/shard_map/attend/pallas_call | solution.py:277
  206.4 0.0 all-to-all-done.3
  206.4 5.8 %all-to-all-start.2 = ((bf16[32,256,128]{2,1,0:T(8,128)(2,1)}), bf16[32,256,128]{2,1,0:T(8,128)(2,1)S(1)}, u32[]{:S(2)}, u32[]{:S(2)}) async-start(bf16[32,256,128]{2,1,0:T(8,128)(2,1)} %bitcast.17), calls=%async_computation.2 | async-start | bytes 4194304 | tf_op jit(solution)/shard_map/all_to_all | solution.py:348
  212.2 65.1 %attend.3 = bf16[32,2,128,128]{3,2,1,0:T(8,128)(2,1)} custom-call(s32[4]{0:T(128)} %get-tuple-element.9.info, s32[4,16]{1,0:T(4,128)} %lengths.3, bf16[32,2,128,128]{3,2,1,0:T(8,128)(2,1)} %bitcast.9.q_ref, bf16[32,256,128]{2,1,0:T(8,128)(2,1)} %copy-done.1, bf16[32,256,128]{2,1,0:T(8,128)(2,1)} %collective-permute-done.other, ...), custom_call_target="tpu_custom_call" | custom-call | flops 21474836480 | bytes 8388608 | tf_op jit(solution)/shard_map/attend/pallas_call | solution.py:277
  277.2 0.0 all-to-all-done.2
  277.2 0.0 copy-start
  277.2 38.0 %all_to_all.26 = bf16[32,256,128]{2,1,0:T(8,128)(2,1)} all-to-all(bf16[32,256,128]{2,1,0:T(8,128)(2,1)} %bitcast.18), channel_id=1, replica_groups=mesh['grp'=4,'cp'=32] {'cp'}, dimensions={0} | all-to-all | bytes 4194304 | tf_op jit(solution)/shard_map/all_to_all | solution.py:348
  315.2 0.0 copy-done
  315.2 4.1 %unpack_outputs.1 = bf16[4,128,4096]{2,1,0:T(8,128)(2,1)} custom-call(bf16[2,16,2,128,128]{4,3,2,1,0:T(8,128)(2,1)} %bitcast.13, bf16[2,16,2,128,128]{4,3,2,1,0:T(8,128)(2,1)} %bitcast.14), custom_call_target="tpu_custom_call" | custom-call | bytes 8388608 | tf_op jit(solution)/shard_map/unpack_outputs/pallas_call | solution.py:350
Async XLA Ops:
  40.8 9.3 %copy-start.1 = (bf16[32,256,128]{2,1,0:T(8,128)(2,1)}, bf16[32,256,128]{2,1,0:T(8,128)(2,1)S(1)}, u32[]{:S(2)}) copy-start(bf16[32,256,128]{2,1,0:T(8,128)(2,1)S(1)} %all_to_all.25.mine) | copy-start | bytes 6291460
  40.8 47.2 %collective-permute-start.1 = (bf16[32,256,128]{2,1,0:T(8,128)(2,1)S(1)}, bf16[32,256,128]{2,1,0:T(8,128)(2,1)}, u32[]{:S(2)}, u32[]{:S(2)}) collective-permute-start(bf16[32,256,128]{2,1,0:T(8,128)(2,1)S(1)} %all_to_all.25.mine), channel_id=1, source_target_pairs={{0,32},{32,64},{64,96},{96,0},{1,33},{33,65},{65,97},{97,1},{2,34}... | collective-permute-start | bytes 6291464 | tf_op jit(solution)/shard_map/ppermute | solution.py:336
  45.5 44.1 %all-to-all-start = ((bf16[32,256,128]{2,1,0:T(8,128)(2,1)}), bf16[32,256,128]{2,1,0:T(8,128)(2,1)}, u32[]{:S(2)}, u32[]{:S(2)}) async-start(bf16[32,256,128]{2,1,0:T(8,128)(2,1)} %bitcast.16), calls=%async_computation | async-start | bytes 4194304 | tf_op jit(solution)/shard_map/all_to_all | solution.py:340
  50.1 44.7 %collective-permute-start = (bf16[32,256,128]{2,1,0:T(8,128)(2,1)S(1)}, bf16[32,256,128]{2,1,0:T(8,128)(2,1)}, u32[]{:S(2)}, u32[]{:S(2)}) collective-permute-start(bf16[32,256,128]{2,1,0:T(8,128)(2,1)S(1)} %all_to_all.25.mine), channel_id=1, source_target_pairs={{0,1},{1,0},{2,3},{3,2},{4,5},{5,4},{6,7},{7,6},{8,9},{9,8},{10,11... | collective-permute-start | bytes 6291464 | tf_op jit(solution)/shard_map/ppermute | solution.py:337
  88.0 6.9 %collective-permute-start.2 = (bf16[32,256,128]{2,1,0:T(8,128)(2,1)}, bf16[32,256,128]{2,1,0:T(8,128)(2,1)}, u32[]{:S(2)}, u32[]{:S(2)}) collective-permute-start(bf16[32,256,128]{2,1,0:T(8,128)(2,1)} %collective-permute-done.1.mine_before), channel_id=1, source_target_pairs={{0,1},{1,0},{2,3},{3,2},{4,5},{5,4},{6,7},{7,6},{8,9},{9,8},{10,11... | collective-permute-start | bytes 6291464 | tf_op jit(solution)/shard_map/ppermute | solution.py:341
  89.6 116.8 %all-to-all-start.3 = ((bf16[32,256,128]{2,1,0:T(8,128)(2,1)}), bf16[32,256,128]{2,1,0:T(8,128)(2,1)}, u32[]{:S(2)}, u32[]{:S(2)}) async-start(bf16[32,256,128]{2,1,0:T(8,128)(2,1)} %bitcast.15), calls=%async_computation.3 | async-start | bytes 4194304 | tf_op jit(solution)/shard_map/all_to_all | solution.py:340
  206.4 70.8 %all-to-all-start.2 = ((bf16[32,256,128]{2,1,0:T(8,128)(2,1)}), bf16[32,256,128]{2,1,0:T(8,128)(2,1)S(1)}, u32[]{:S(2)}, u32[]{:S(2)}) async-start(bf16[32,256,128]{2,1,0:T(8,128)(2,1)} %bitcast.17), calls=%async_computation.2 | async-start | bytes 4194304 | tf_op jit(solution)/shard_map/all_to_all | solution.py:348
  277.2 38.0 %copy-start = (bf16[32,256,128]{2,1,0:T(8,128)(2,1)}, bf16[32,256,128]{2,1,0:T(8,128)(2,1)S(1)}, u32[]{:S(2)}) copy-start(bf16[32,256,128]{2,1,0:T(8,128)(2,1)S(1)} %all-to-all-done.2) | copy-start | bytes 6291460
where the time goes:
time: 320 us; the launch traced here: 319 us
  Pallas kernels  189 us (59%)
  blocking collectives  74.7 us (23%)
  waiting for transfers between devices  37.5 us (12%)
  starting transfers between devices  16.2 us (5%)
    pallas_call x2, Pallas kernels, attention(): pl.pallas_call(attend, grid_spec=pltpu.PrefetchScalarGridSpec(num_scalar_...  177 us
    all_to_all x1, blocking collectives, on_device(): lax.all_to_all(result.reshape(RANKS, 2 * BLOCK, WIDTH), 'cp', 0, 0, tiled...  38 us
    ppermute x1, waiting for transfers between devices, on_device(): mine_before = lax.ppermute(mine, 'grp', onward)  37.5 us
    all_to_all x1, blocking collectives, on_device(): lax.all_to_all(packed_kv.reshape(RANKS, 2 * BLOCK, WIDTH), 'cp', 0, 0, ti...  36.7 us
    all_to_all x2, starting transfers between devices, on_device(): lax.all_to_all(packed.reshape(RANKS, 2 * BLOCK, WIDTH), 'cp', 0, 0, tiled...  9.1 us
  transfers between devices with their start and end apart: 6, of which 1 were waited for; matrix products, arithmetic and copies ran while one was open for 0% of the time, Pallas kernels for 57%

commit v1 on v0

--- a/solution.py
+++ b/solution.py
@@ -30,20 +30,42 @@
         out_ref[0, head, 0, 1] = v_ref[0, :, columns]
 
 
-def pack_queries(q_ref, even_ref, odd_ref):
-    for turn, out_ref in enumerate((even_ref, odd_ref)):
+def swapped(info, lengths, pair):
+    plane = info[1]
+
+    def work(stream):
+        total, begin = 0, 0
+        for doc in range(DOCS):
+            length = lengths[stream, doc]
+            low = jnp.maximum(plane * CHUNK - begin, 0)
+            high = jnp.minimum((plane + 1) * CHUNK - begin, length)
+            total += jnp.where(high > low, high * high - low * low, 0)
+            begin += length
+        return total
+
+    return (work(2 * pair + 1) > work(2 * pair)).astype(jnp.int32)
+
+
+def pack_queries(info, lengths, q_ref, first_ref, second_ref):
+    swap = swapped(info, lengths, pl.program_id(0))
+    for turn, out_ref in enumerate((first_ref, second_ref)):
+        stream = jnp.where(swap == 1, 1 - turn, turn)
         for head in range(QUERY_HEADS):
-            out_ref[0, head // 2, head % 2] = q_ref[turn, :, head * WIDTH : (head + 1) * WIDTH]
-
-
-def unpack_outputs(even_ref, odd_ref, out_ref):
-    for turn, in_ref in enumerate((even_ref, odd_ref)):
+            out_ref[0, head // 2, head % 2] = q_ref[stream, :, head * WIDTH : (head + 1) * WIDTH]
+
+
+def unpack_outputs(info, lengths, first_ref, second_ref, out_ref):
+    swap = swapped(info, lengths, pl.program_id(0))
+    for turn, in_ref in enumerate((first_ref, second_ref)):
+        stream = jnp.where(swap == 1, 1 - turn, turn)
         for head in range(QUERY_HEADS):
-            out_ref[turn, :, head * WIDTH : (head + 1) * WIDTH] = in_ref[0, head // 2, head % 2]
+            out_ref[stream, :, head * WIDTH : (head + 1) * WIDTH] = in_ref[0, head // 2, head % 2]
 
 
 def attend(info, lengths, q_ref, mine, other, mine_before, other_before, o_ref, kbuf, vbuf, probs, acc, sums, portion, lows, reach, top, ends, low_of, whole_of, docs_of, span_of, arrived):
-    core, plane, pair, turn = info[0], info[1], info[2], info[3]
+    core, plane, pair = info[0], info[1], info[2]
+    swap = swapped(info, lengths, pair)
+    turn = jnp.where(swap == 1, 1 - info[3], info[3])
     stream = pair * 2 + turn
     base = (plane - 1) * CHUNK
 
@@ -320,15 +342,19 @@
         cost_estimate=estimate(0, 4 << 20),
         name="pack_keys",
     )(keys, values)
+    infos = [jnp.stack([rank % 2, plane, rank // 16, jnp.int32(turn)]).astype(jnp.int32) for turn in range(2)]
     packed_q = pl.pallas_call(
         pack_queries,
-        grid=(2,),
-        in_specs=[pl.BlockSpec((2, BLOCK, QUERY_HEADS * WIDTH), lambda p: (p, 0, 0))],
-        out_specs=[pl.BlockSpec((1, 16, 2, BLOCK, WIDTH), lambda p: (p, 0, 0, 0, 0))] * 2,
+        grid_spec=pltpu.PrefetchScalarGridSpec(
+            num_scalar_prefetch=2,
+            grid=(2,),
+            in_specs=[pl.BlockSpec((2, BLOCK, QUERY_HEADS * WIDTH), lambda p, *_: (p, 0, 0))],
+            out_specs=[pl.BlockSpec((1, 16, 2, BLOCK, WIDTH), lambda p, *_: (p, 0, 0, 0, 0))] * 2,
+        ),
         out_shape=[jax.ShapeDtypeStruct((2, 16, 2, BLOCK, WIDTH), bf16)] * 2,
         cost_estimate=estimate(0, 8 << 20),
         name="pack_queries",
-    )(queries)
+    )(infos[0], doc_lengths, queries)
 
     swap = [(i, i ^ 1) for i in range(RANKS)]
     onward = [(i, (i + 1) % 4) for i in range(4)]
@@ -341,21 +367,23 @@
     other_before = lax.ppermute(mine_before, "cp", swap)
     back = []
     for turn in range(2):
-        info = jnp.stack([rank % 2, plane, rank // 16, turn]).astype(jnp.int32)
         result = attention(
-            info, doc_lengths, got_q[turn].reshape(RANKS, 2, BLOCK, WIDTH), mine, other, mine_before, other_before
+            infos[turn], doc_lengths, got_q[turn].reshape(RANKS, 2, BLOCK, WIDTH), mine, other, mine_before, other_before
         )
         sent = lax.all_to_all(result.reshape(RANKS, 2 * BLOCK, WIDTH), "cp", 0, 0, tiled=True)
         back.append(sent.reshape(2, 16, 2, BLOCK, WIDTH))
     return pl.pallas_call(
         unpack_outputs,
-        grid=(2,),
-        in_specs=[pl.BlockSpec((1, 16, 2, BLOCK, WIDTH), lambda p: (p, 0, 0, 0, 0))] * 2,
-        out_specs=pl.BlockSpec((2, BLOCK, QUERY_HEADS * WIDTH), lambda p: (p, 0, 0)),
+        grid_spec=pltpu.PrefetchScalarGridSpec(
+            num_scalar_prefetch=2,
+            grid=(2,),
+            in_specs=[pl.BlockSpec((1, 16, 2, BLOCK, WIDTH), lambda p, *_: (p, 0, 0, 0, 0))] * 2,
+            out_specs=pl.BlockSpec((2, BLOCK, QUERY_HEADS * WIDTH), lambda p, *_: (p, 0, 0)),
+        ),
         out_shape=jax.ShapeDtypeStruct((4, BLOCK, QUERY_HEADS * WIDTH), bf16),
         cost_estimate=estimate(0, 8 << 20),
         name="unpack_outputs",
-    )(*back)
+    )(infos[0], doc_lengths, *back)
 
 
 def solution(mesh):

time: 320 us -> 360 us (1.12)
  the two profiles are of different devices: /device:TPU:25 before, /device:TPU:17 now
where the time goes in v1:
time: 360 us; the launch traced here: 359 us
  blocking collectives  182 us (51%)
  Pallas kernels  118 us (33%)
  waiting for transfers between devices  45.1 us (13%)
  starting transfers between devices  12.8 us (4%)
    all_to_all x1, blocking collectives, on_device(): lax.all_to_all(result.reshape(RANKS, 2 * BLOCK, WIDTH), 'cp', 0, 0, tiled...  113 us
    pallas_call x2, Pallas kernels, attention(): pl.pallas_call(attend, grid_spec=pltpu.PrefetchScalarGridSpec(num_scalar_...  104 us
    ppermute x1, waiting for transfers between devices, on_device(): mine_before = lax.ppermute(mine, 'grp', onward)  45.1 us
    all_to_all x1, blocking collectives, on_device(): lax.all_to_all(packed_kv.reshape(RANKS, 2 * BLOCK, WIDTH), 'cp', 0, 0, ti...  36.7 us
    all_to_all x1, blocking collectives, on_device(): lax.all_to_all(packed.reshape(RANKS, 2 * BLOCK, WIDTH), 'cp', 0, 0, tiled...  32.6 us
  transfers between devices with their start and end apart: 5, of which 1 were waited for; matrix products, arithmetic and copies ran while one was open for 0% of the time, Pallas kernels for 30%

profile of v1, /device:TPU:17, one launch (start us, length us, event | category | flops | bytes accessed | tf_op | source)
XLA Modules:
  0.0 359.0 jit_solution(17427066546469726258)
XLA Ops:
  0.0 4.0 %pack_keys.1 = bf16[2,8,2,2,128,128]{5,4,3,2,1,0:T(8,128)(2,1)} custom-call(bf16[4,128,1024]{2,1,0:T(8,128)(2,1)} %k_ref.1, bf16[4,128,1024]{2,1,0:T(8,128)(2,1)} %v_ref.1), custom_call_target="tpu_custom_call" | custom-call | bytes 4194304 | tf_op jit(solution)/shard_map/pack_keys/pallas_call | solution.py:336
  4.0 36.7 %all_to_all.25.mine = bf16[32,256,128]{2,1,0:T(8,128)(2,1)S(1)} all-to-all(bf16[32,256,128]{2,1,0:T(8,128)(2,1)} %bitcast.14), channel_id=1, replica_groups=mesh['grp'=4,'cp'=32] {'cp'}, dimensions={0} | all-to-all | bytes 4194304 | tf_op jit(solution)/shard_map/all_to_all | solution.py:361
  40.8 0.0 copy-start.1
  40.8 1.0 collective-permute-start.1
  41.8 0.7 pad_add_fusion.2
  42.4 0.4 collective-permute-start
  42.8 45.1 %collective-permute-done.1.mine_before = bf16[32,256,128]{2,1,0:T(8,128)(2,1)} collective-permute-done((bf16[32,256,128]{2,1,0:T(8,128)(2,1)S(1)}, bf16[32,256,128]{2,1,0:T(8,128)(2,1)}, u32[]{:S(2)}, u32[]{:S(2)}) %collective-permute-start.1) | collective-permute-done | bytes 2097184 | tf_op jit(solution)/shard_map/ppermute | solution.py:362
  88.0 1.0 collective-permute-start.2
  88.9 0.6 pad_add_fusion.info
  89.5 4.7 %pack_queries.1 = (bf16[2,16,2,128,128]{4,3,2,1,0:T(8,128)(2,1)}, bf16[2,16,2,128,128]{4,3,2,1,0:T(8,128)(2,1)}) custom-call(s32[4]{0:T(128)} %pad_add_fusion.info, s32[4,16]{1,0:T(4,128)} %lengths.7, bf16[4,128,4096]{2,1,0:T(8,128)(2,1)} %q_ref.1), custom_call_target="tpu_custom_call" | custom-call | bytes 8388608 | tf_op jit(solution)/shard_map/pack_queries/pallas_call | solution.py:346
  94.2 0.0 copy-done.1
  94.2 32.6 %all_to_all.26 = bf16[32,256,128]{2,1,0:T(8,128)(2,1)} all-to-all(bf16[32,256,128]{2,1,0:T(8,128)(2,1)} %bitcast.19), channel_id=1, replica_groups=mesh['grp'=4,'cp'=32] {'cp'}, dimensions={0} | all-to-all | bytes 4194304 | tf_op jit(solution)/shard_map/all_to_all | solution.py:366
  126.8 4.6 %all-to-all-start = ((bf16[32,256,128]{2,1,0:T(8,128)(2,1)}), bf16[32,256,128]{2,1,0:T(8,128)(2,1)}, u32[]{:S(2)}, u32[]{:S(2)}) async-start(bf16[32,256,128]{2,1,0:T(8,128)(2,1)} %bitcast.15), calls=%async_computation | async-start | bytes 4194304 | tf_op jit(solution)/shard_map/all_to_all | solution.py:366
  131.3 0.0 collective-permute-done.other
  131.3 0.0 collective-permute-done.2.other_before
  131.4 69.4 %attend.3 = bf16[32,2,128,128]{3,2,1,0:T(8,128)(2,1)} custom-call(s32[4]{0:T(128)} %get-tuple-element.9.info, s32[4,16]{1,0:T(4,128)} %lengths.7, bf16[32,2,128,128]{3,2,1,0:T(8,128)(2,1)} %bitcast.17, bf16[32,256,128]{2,1,0:T(8,128)(2,1)} %copy-done.1, bf16[32,256,128]{2,1,0:T(8,128)(2,1)} %collective-permute-done.other, ...), custom_call_target="tpu_custom_call" | custom-call | flops 21474836480 | bytes 8388608 | tf_op jit(solution)/shard_map/attend/pallas_call | solution.py:299
  200.8 0.0 all-to-all-done
  200.8 5.8 %all-to-all-start.4 = ((bf16[32,256,128]{2,1,0:T(8,128)(2,1)}), bf16[32,256,128]{2,1,0:T(8,128)(2,1)S(1)}, u32[]{:S(2)}, u32[]{:S(2)}) async-start(bf16[32,256,128]{2,1,0:T(8,128)(2,1)} %bitcast.16), calls=%async_computation.4 | async-start | bytes 4194304 | tf_op jit(solution)/shard_map/all_to_all | solution.py:373
  206.7 34.6 %attend.2 = bf16[32,2,128,128]{3,2,1,0:T(8,128)(2,1)} custom-call(s32[4]{0:T(128)} %pad_add_fusion.info, s32[4,16]{1,0:T(4,128)} %lengths.7, bf16[32,2,128,128]{3,2,1,0:T(8,128)(2,1)} %bitcast.4.q_ref, bf16[32,256,128]{2,1,0:T(8,128)(2,1)} %copy-done.1, bf16[32,256,128]{2,1,0:T(8,128)(2,1)} %collective-permute-done.other, ...), custom_call_target="tpu_custom_call" | custom-call | flops 21474836480 | bytes 8388608 | tf_op jit(solution)/shard_map/attend/pallas_call | solution.py:299
  241.3 0.0 all-to-all-done.4
  241.3 0.0 copy-start
  241.3 112.8 %all_to_all.27 = bf16[32,256,128]{2,1,0:T(8,128)(2,1)} all-to-all(bf16[32,256,128]{2,1,0:T(8,128)(2,1)} %bitcast.18), channel_id=1, replica_groups=mesh['grp'=4,'cp'=32] {'cp'}, dimensions={0} | all-to-all | bytes 4194304 | tf_op jit(solution)/shard_map/all_to_all | solution.py:373
  354.1 0.0 copy-done
  354.2 4.9 %unpack_outputs.1 = bf16[4,128,4096]{2,1,0:T(8,128)(2,1)} custom-call(s32[4]{0:T(128)} %pad_add_fusion.info, s32[4,16]{1,0:T(4,128)} %lengths.7, bf16[2,16,2,128,128]{4,3,2,1,0:T(8,128)(2,1)} %bitcast.13, bf16[2,16,2,128,128]{4,3,2,1,0:T(8,128)(2,1)} %bitcast.12), custom_call_target="tpu_custom_call" | custom-call | bytes 8388608 | tf_op jit(solution)/shard_map/unpack_outputs/pallas_call | solution.py:375
Async XLA Ops:
  40.8 53.4 %copy-start.1 = (bf16[32,256,128]{2,1,0:T(8,128)(2,1)}, bf16[32,256,128]{2,1,0:T(8,128)(2,1)S(1)}, u32[]{:S(2)}) copy-start(bf16[32,256,128]{2,1,0:T(8,128)(2,1)S(1)} %all_to_all.25.mine) | copy-start | bytes 6291460
  40.8 47.2 %collective-permute-start.1 = (bf16[32,256,128]{2,1,0:T(8,128)(2,1)S(1)}, bf16[32,256,128]{2,1,0:T(8,128)(2,1)}, u32[]{:S(2)}, u32[]{:S(2)}) collective-permute-start(bf16[32,256,128]{2,1,0:T(8,128)(2,1)S(1)} %all_to_all.25.mine), channel_id=1, source_target_pairs={{0,32},{32,64},{64,96},{96,0},{1,33},{33,65},{65,97},{97,1},{2,34}... | collective-permute-start | bytes 6291464 | tf_op jit(solution)/shard_map/ppermute | solution.py:362
  42.4 88.9 %collective-permute-start = (bf16[32,256,128]{2,1,0:T(8,128)(2,1)S(1)}, bf16[32,256,128]{2,1,0:T(8,128)(2,1)}, u32[]{:S(2)}, u32[]{:S(2)}) collective-permute-start(bf16[32,256,128]{2,1,0:T(8,128)(2,1)S(1)} %all_to_all.25.mine), channel_id=1, source_target_pairs={{0,1},{1,0},{2,3},{3,2},{4,5},{5,4},{6,7},{7,6},{8,9},{9,8},{10,11... | collective-permute-start | bytes 6291464 | tf_op jit(solution)/shard_map/ppermute | solution.py:363
  88.0 43.4 %collective-permute-start.2 = (bf16[32,256,128]{2,1,0:T(8,128)(2,1)}, bf16[32,256,128]{2,1,0:T(8,128)(2,1)}, u32[]{:S(2)}, u32[]{:S(2)}) collective-permute-start(bf16[32,256,128]{2,1,0:T(8,128)(2,1)} %collective-permute-done.1.mine_before), channel_id=1, source_target_pairs={{0,1},{1,0},{2,3},{3,2},{4,5},{5,4},{6,7},{7,6},{8,9},{9,8},{10,11... | collective-permute-start | bytes 6291464 | tf_op jit(solution)/shard_map/ppermute | solution.py:367
  126.8 74.0 %all-to-all-start = ((bf16[32,256,128]{2,1,0:T(8,128)(2,1)}), bf16[32,256,128]{2,1,0:T(8,128)(2,1)}, u32[]{:S(2)}, u32[]{:S(2)}) async-start(bf16[32,256,128]{2,1,0:T(8,128)(2,1)} %bitcast.15), calls=%async_computation | async-start | bytes 4194304 | tf_op jit(solution)/shard_map/all_to_all | solution.py:366
  200.8 40.5 %all-to-all-start.4 = ((bf16[32,256,128]{2,1,0:T(8,128)(2,1)}), bf16[32,256,128]{2,1,0:T(8,128)(2,1)S(1)}, u32[]{:S(2)}, u32[]{:S(2)}) async-start(bf16[32,256,128]{2,1,0:T(8,128)(2,1)} %bitcast.16), calls=%async_computation.4 | async-start | bytes 4194304 | tf_op jit(solution)/shard_map/all_to_all | solution.py:373
  241.3 112.8 %copy-start = (bf16[32,256,128]{2,1,0:T(8,128)(2,1)}, bf16[32,256,128]{2,1,0:T(8,128)(2,1)S(1)}, u32[]{:S(2)}) copy-start(bf16[32,256,128]{2,1,0:T(8,128)(2,1)S(1)} %all-to-all-done.4) | copy-start | bytes 6291460
